TPU v7x, 32 devices: a whole 2x2x4 slice. The times are simulated.
32 devices in a mesh: seq: 4 (over y, x), span: 4 (over z), kvg: 2 (over core).
Axes of the slice: x: 2, y: 2, z: 4, core: 2. Of those that a mesh axis runs over, the one named last changes fastest.
Arguments:
- query_rows: bfloat16 [8704, 1792], P(('seq', 'span'), 'kvg'), parts along dimension 0, may hold values from -256 to 256
- key_rows: bfloat16 [8704, 256], P(('seq', 'span'), 'kvg'), parts along dimension 0, may hold values from -6 to 6
- value_rows: bfloat16 [8704, 256], P(('seq', 'span'), 'kvg'), parts along dimension 0, may hold values from -6 to 6
- out_grad: bfloat16 [8704, 1792], P(('seq', 'span'), 'kvg'), parts along dimension 0, may hold values from -6 to 6
- ratios: int32 [16], P('seq'), parts along dimension 0, may hold values from 16 to 64, as said below
Outputs:
- attended: bfloat16 [8704, 1792], P(('seq', 'span'), 'kvg'), parts along dimension 0
- query_grad: bfloat16 [8704, 1792], P(('seq', 'span'), 'kvg'), parts along dimension 0
- key_grad: bfloat16 [8704, 256], P(('seq', 'span'), 'kvg'), parts along dimension 0
- value_grad: bfloat16 [8704, 256], P(('seq', 'span'), 'kvg'), parts along dimension 0
There are 4 independent parts, one for each index of `seq`. A program takes and returns all parts, laid end to end along the dimension named above; each array names one. Nothing has to cross between parts.
Inputs may be any that keep to these rules, and one draw needn't show every extreme that they name: `ratios`: every ratio is 16, 32 or 64, and some span of every sequence has 16.
All inputs are finite; a program needn't handle non-finite values.
Results may differ from a plain program's by a relative error of at most 0.0096.
Values may be sent and summed in bfloat16 or wider, within the bound.
A program may use at most 64 MiB of HBM per device.

v0:
```python
import jax
import jax.numpy as jnp
from jax import lax
from jax.sharding import PartitionSpec as P

SPAN = 512
HD = 128
QPG = 7
BMAX = 32
SEG = 544
floor_score = -1e30


def product(pattern, first_arg, second_arg):
    return jnp.einsum(pattern, first_arg, second_arg, preferred_element_type=jnp.float32)


def build_masks(ratios, first_span, local_spans):
    counts = SPAN // ratios
    slot_ids = jnp.arange(BMAX, dtype=jnp.int32)
    live_slots = (slot_ids[None, :] < counts[:, None]).reshape(-1)
    span_ids = first_span + jnp.arange(local_spans, dtype=jnp.int32)
    owner_span = jnp.arange(live_slots.shape[0], dtype=jnp.int32) // BMAX
    beacon_mask = (owner_span[None, :] < span_ids[:, None]) & live_slots[None, :]
    local_ratio = lax.dynamic_slice_in_dim(ratios, first_span, local_spans)
    local_count = SPAN // local_ratio
    positions = jnp.arange(SEG, dtype=jnp.int32)
    is_beacon = positions >= SPAN
    slot_of = positions - SPAN
    key_order = jnp.where(
        is_beacon[None, :], (slot_of[None, :] + 1) * local_ratio[:, None] - 1, positions[None, :]
    )
    live_row = jnp.logical_not(is_beacon[None, :]) | (slot_of[None, :] < local_count[:, None])
    raw_key = jnp.logical_not(is_beacon)[None, None, :] & (
        key_order[:, None, :] <= key_order[:, :, None]
    )
    beacon_key = (
        is_beacon[None, :, None]
        & is_beacon[None, None, :]
        & live_row[:, None, :]
        & (positions[None, None, :] <= positions[None, :, None])
    )
    return (beacon_mask, raw_key | beacon_key, live_row.astype(jnp.float32))


def attend_head(
    query_head,
    grad_head,
    beacon_keys,
    beacon_values,
    own_keys,
    own_values,
    beacon_mask,
    own_mask,
    live_rows,
):
    score_scale = HD ** (-0.5)
    beacon_scores = jnp.where(
        beacon_mask[:, None, :],
        product("csd,bd->csb", query_head, beacon_keys) * score_scale,
        floor_score,
    )
    own_scores = jnp.where(
        own_mask, product("csd,ctd->cst", query_head, own_keys) * score_scale, floor_score
    )
    row_top = jnp.maximum(jnp.max(beacon_scores, -1), jnp.max(own_scores, -1))
    row_total = jnp.sum(jnp.exp(beacon_scores - row_top[..., None]), -1) + jnp.sum(
        jnp.exp(own_scores - row_top[..., None]), -1
    )
    row_lse = row_top + jnp.log(row_total)
    beacon_probs = jnp.exp(beacon_scores - row_lse[..., None])
    own_probs = jnp.exp(own_scores - row_lse[..., None])
    beacon_weights = beacon_probs.astype(jnp.bfloat16)
    own_weights = own_probs.astype(jnp.bfloat16)
    mixed_rows = product("csb,bd->csd", beacon_weights, beacon_values) + product(
        "cst,ctd->csd", own_weights, own_values
    )
    attended = (mixed_rows * live_rows[..., None]).astype(jnp.bfloat16)
    grad_rows = grad_head * live_rows.astype(jnp.bfloat16)[..., None]
    row_delta = jnp.sum(grad_rows.astype(jnp.float32) * attended.astype(jnp.float32), -1)
    beacon_sgrad = (
        beacon_probs * (product("csd,bd->csb", grad_rows, beacon_values) - row_delta[..., None])
    ).astype(jnp.bfloat16)
    own_sgrad = (
        own_probs * (product("csd,ctd->cst", grad_rows, own_values) - row_delta[..., None])
    ).astype(jnp.bfloat16)
    query_grad = (
        score_scale
        * (
            product("csb,bd->csd", beacon_sgrad, beacon_keys)
            + product("cst,ctd->csd", own_sgrad, own_keys)
        )
    ).astype(jnp.bfloat16)
    beacon_kgrad = score_scale * product("csb,csd->bd", beacon_sgrad, query_head)
    beacon_vgrad = product("csb,csd->bd", beacon_weights, grad_rows)
    own_kgrad = score_scale * product("cst,csd->ctd", own_sgrad, query_head)
    own_vgrad = product("cst,csd->ctd", own_weights, grad_rows)
    return (attended, query_grad, beacon_kgrad, beacon_vgrad, own_kgrad, own_vgrad)


def local(query_rows, key_rows, value_rows, out_grad, ratios):
    span_index = lax.axis_index("span")
    local_spans = query_rows.shape[0] // SEG
    groups = key_rows.shape[1] // HD
    beacon_count = ratios.shape[0] * BMAX
    first_span = span_index * local_spans
    beacon_mask, own_mask, live_rows = build_masks(ratios, first_span, local_spans)
    query_blocks = query_rows.reshape(local_spans, SEG, groups, QPG, HD)
    grad_blocks = out_grad.reshape(local_spans, SEG, groups, QPG, HD)
    key_blocks = key_rows.reshape(local_spans, SEG, groups, HD)
    value_blocks = value_rows.reshape(local_spans, SEG, groups, HD)
    own_pair = jnp.concatenate(
        [
            key_blocks[:, SPAN:].reshape(local_spans * BMAX, groups * HD),
            value_blocks[:, SPAN:].reshape(local_spans * BMAX, groups * HD),
        ],
        1,
    )
    beacon_pairs = lax.all_gather(own_pair, "span", axis=0, tiled=True)
    attended_parts, query_parts, term_keys, term_values, own_key_parts, own_value_parts = (
        [],
        [],
        [],
        [],
        [],
        [],
    )
    own_keys = key_blocks[:, :, 0]
    own_values = value_blocks[:, :, 0]
    beacon_keys = beacon_pairs[:, 0:HD]
    beacon_values = beacon_pairs[:, groups * HD : (groups + 1) * HD]
    beacon_ksum = jnp.zeros((beacon_count, HD), jnp.float32)
    beacon_vsum = jnp.zeros((beacon_count, HD), jnp.float32)
    own_ksum = jnp.zeros((local_spans, SEG, HD), jnp.float32)
    own_vsum = jnp.zeros((local_spans, SEG, HD), jnp.float32)
    head_outputs = []
    head_grads = []
    for head_index in range(QPG):
        result = attend_head(
            query_blocks[:, :, 0, head_index],
            grad_blocks[:, :, 0, head_index],
            beacon_keys,
            beacon_values,
            own_keys,
            own_values,
            beacon_mask,
            own_mask,
            live_rows,
        )
        head_outputs.append(result[0])
        head_grads.append(result[1])
        beacon_ksum = beacon_ksum + result[2]
        beacon_vsum = beacon_vsum + result[3]
        own_ksum = own_ksum + result[4]
        own_vsum = own_vsum + result[5]
    attended_parts.append(jnp.stack(head_outputs, 2))
    query_parts.append(jnp.stack(head_grads, 2))
    term_keys.append(beacon_ksum)
    term_values.append(beacon_vsum)
    own_key_parts.append(own_ksum)
    own_value_parts.append(own_vsum)
    grad_term = jnp.concatenate(term_keys + term_values, 1)
    own_sums = lax.psum_scatter(grad_term, "span", scatter_dimension=0, tiled=True)
    own_sums = own_sums.reshape(local_spans, BMAX, 2 * groups, HD)
    own_key = jnp.stack(own_key_parts, 2)
    own_value = jnp.stack(own_value_parts, 2)
    key_total = jnp.concatenate([own_key[:, :SPAN], own_key[:, SPAN:] + own_sums[:, :, :groups]], 1)
    value_total = jnp.concatenate(
        [own_value[:, :SPAN], own_value[:, SPAN:] + own_sums[:, :, groups:]], 1
    )
    attended = jnp.stack(attended_parts, 2).reshape(local_spans * SEG, groups * QPG * HD)
    query_grad = jnp.stack(query_parts, 2).reshape(local_spans * SEG, groups * QPG * HD)
    key_grad = key_total.astype(jnp.bfloat16).reshape(local_spans * SEG, groups * HD)
    value_grad = value_total.astype(jnp.bfloat16).reshape(local_spans * SEG, groups * HD)
    return (attended, query_grad, key_grad, value_grad)


def solution(mesh):
    placed = (
        P(("seq", "span"), "kvg"),
        P(("seq", "span"), "kvg"),
        P(("seq", "span"), "kvg"),
        P(("seq", "span"), "kvg"),
        P("seq"),
    )
    return jax.shard_map(
        local,
        mesh=mesh,
        in_specs=placed,
        out_specs=(
            P(("seq", "span"), "kvg"),
            P(("seq", "span"), "kvg"),
            P(("seq", "span"), "kvg"),
            P(("seq", "span"), "kvg"),
        ),
        check_vma=False,
    )
```

profile of v0, /device:TPU:0, one launch (start us, length us, event | category | flops | bytes accessed | tf_op | source)
XLA Modules:
  0.0 112.2 jit_solution(4719098975755676397)
XLA Ops:
  7.2 1.2 %dynamic_slice.3 = s32[1]{0:T(128)} dynamic-slice(s32[4]{0:T(128)} %param.9, s32[]{:T(128)S(6)} %select_n.105), dynamic_slice_sizes={1} | dynamic-slice | bytes 12 | tf_op jit(solution)/shard_map/dynamic_slice | solution.py:25
  10.4 0.8 and_select_fusion
  11.9 2.2 %reshape.1308 = bf16[1,544,1,7,128]{4,3,1,2,0:T(8,128)(2,1)S(1)} reshape(bf16[544,896]{1,0:T(8,128)(2,1)} %param.5) | data formatting | bytes 1949696 | tf_op jit(solution)/shard_map/reshape | solution.py:108
  14.2 2.4 %fusion.265 = (bf16[1,544,1,1,128]{4,3,1,2,0:T(2,128)(2,1)S(1)}, bf16[1,544,1,1,128]{4,3,1,2,0:T(2,128)(2,1)S(1)}, bf16[1,544,1,1,128]{4,3,1,2,0:T(2,128)(2,1)},...) fusion(bf16[1,544,1,7,128]{4,3,1,2,0:T(8,128)(2,1)S(1)} %reshap, ...), kind=kLoop, calls=%fused_computation.404 | loop fusion | bytes 1949696 | tf_op jit(solution)/shard_map/slice | solution.py:140
  16.6 15.1 %all_gather.3 = bf16[128,256]{1,0:T(8,128)(2,1)S(1)} all-gather(bf16[32,256]{1,0:T(8,128)(2,1)S(1)} %pad_maximum_fusion.3), channel_id=1, replica_groups=mesh['seq'=4,'span'=4,'kvg'=2] {'span'}, dimensions={0}, use_global_device_ids=true | all-gather | bytes 81920 | tf_op jit(solution)/shard_map/all_gather | solution.py:119
  32.6 1.4 %fusion.278 = (f32[544]{0:T(1024)S(1)}, f32[544,544]{0,1:T(8,128)S(1)}) fusion(bf16[544,128]{1,0:T(8,128)(2,1)S(1)} %copy-done.16, bf16[1,544,1,1,128]{4,1,3,2,0:T(8,128)(2,1)S(1)} %copy.71, pred[544]{0:T(1024)(128)(4,1)} %copy-done.124, pred[544]{0:T(1024)(128)(4,1)S(1)} %get-tuple-element.80, s32[544]{0:T(1024)S(1)} %iota_select_fusion, ...), kind=kOutput, calls=%fused_computation.417 | convolution fusion | flops 78718432 | bytes 1468256 | tf_op jit(solution)/shard_map/csd,ctd->cst/dot_general | solution.py:15
  34.8 1.4 %fusion.276 = (f32[544]{0:T(1024)S(1)}, f32[544,544]{0,1:T(8,128)S(1)}) fusion(bf16[544,128]{1,0:T(8,128)(2,1)S(1)} %copy-done.16, bf16[1,544,1,1,128]{4,1,3,2,0:T(8,128)(2,1)S(1)} %copy.70, pred[544]{0:T(1024)(128)(4,1)S(1)} %copy-done.125, pred[544]{0:T(1024)(128)(4,1)} %copy-done.122, s32[544]{0:T(1024)S(1)} %iota_select_fusion, ...), kind=kOutput, calls=%fused_computation.415 | convolution fusion | flops 78718432 | bytes 1468256 | tf_op jit(solution)/shard_map/csd,ctd->cst/dot_general | solution.py:15
  42.4 1.0 fusion.229
  43.9 1.0 fusion.231
  45.4 1.0 fusion.233
  47.0 1.0 fusion.235
  48.5 1.0 fusion.237
  50.0 1.0 fusion.239
  52.1 1.0 fusion.241
  53.0 3.0 %reshape.1316 = bf16[1,544,1,7,128]{4,3,1,2,0:T(8,128)(2,1)} reshape(bf16[544,896]{1,0:T(8,128)(2,1)} %param.8) | data formatting | bytes 1949696 | tf_op jit(solution)/shard_map/reshape | solution.py:109
  56.1 6.1 %fusion.264 = (bf16[1,544,1,1,128]{4,3,1,2,0:T(2,128)(2,1)S(1)}, bf16[1,544,1,1,128]{4,3,1,2,0:T(2,128)(2,1)S(1)}, bf16[1,544,1,1,128]{4,3,1,2,0:T(2,128)(2,1)S(...) fusion(bf16[1,544,1,7,128]{4,3,1,2,0:T(8,128)(2,1)} %reshape.1316), kind=kLoop, calls=%fused_computation.403 | loop fusion | bytes 1949696 | tf_op jit(solution)/shard_map/slice | solution.py:141
  62.7 0.8 copy-done.11
  64.7 0.7 copy-done.5
  68.1 0.9 copy-done.61
  69.1 0.9 multiply_reduce_fusion
  78.1 0.8 copy.64
  78.9 1.9 %fusion.109 = f32[544,128]{1,0:T(8,128)S(1)} fusion(f32[544,544]{0,1:T(8,128)} %copy-done.13, f32[544]{0:T(1024)S(1)} %copy-done.109, bf16[1,544,1,1,128]{4,1,3,2,0:T(8,128)(2,1)S(1)} %copy-done.60, bf16[544]{0:T(1024)(128)(2,1)S(1)} %get-tuple-element.76), kind=kOutput, calls=%fused_computation.210 | convolution fusion | flops 76421120 | bytes 1604800 | tf_op jit(solution)/shard_map/cst,csd->ctd/dot_general | solution.py:15
  81.4 0.8 copy-done.12
  82.7 0.8 copy-done.9
  84.1 0.8 copy-done.6
  85.4 0.9 copy-done.3
  87.2 0.7 fusion.17
  99.9 1.1 copy.93
  101.8 1.1 copy.94
  102.9 0.9 copy.65
  104.0 0.7 pad_maximum_fusion.1
  104.6 0.7 pad_maximum_fusion
  (379 shorter events, 39.0 us)
Async XLA Ops:
  7.2 95.8 %reduce-scatter.4.cloned.1.call-start = ((), (), s32[]{:S(2)}) async-start(), calls=%async_computation.1 | async-start | bytes 163840
  10.4 21.5 %copy-start.126 = (pred[544]{0:T(1024)(128)(4,1)}, pred[544]{0:T(1024)(128)(4,1)S(1)}, u32[]{:S(2)}) copy-start(pred[544]{0:T(1024)(128)(4,1)S(1)} %fusion.220) | copy-start | bytes 1636
  11.3 20.7 %copy-start.124 = (pred[544]{0:T(1024)(128)(4,1)}, pred[544]{0:T(1024)(128)(4,1)S(1)}, u32[]{:S(2)}) copy-start(pred[544]{0:T(1024)(128)(4,1)S(1)} %get-tuple-element.81) | copy-start | bytes 1636
  11.3 21.3 %copy-start.122 = (pred[544]{0:T(1024)(128)(4,1)}, pred[544]{0:T(1024)(128)(4,1)S(1)}, u32[]{:S(2)}) copy-start(pred[544]{0:T(1024)(128)(4,1)S(1)} %get-tuple-element.80) | copy-start | bytes 1636
  16.6 17.4 %copy-start.29 = (bf16[1,544,1,1,128]{4,1,3,2,0:T(8,128)(2,1)}, bf16[1,544,1,1,128]{4,1,3,2,0:T(8,128)(2,1)S(1)}, u32[]{:S(2)}) copy-start(bf16[1,544,1,1,128]{4,1,3,2,0:T(8,128)(2,1)S(1)} %copy.72) | copy-start | bytes 417796
  34.7 9.2 %copy-start.17 = (f32[128,544]{0,1:T(8,128)}, f32[128,544]{0,1:T(8,128)S(1)}, u32[]{:S(2)}) copy-start(f32[128,544]{0,1:T(8,128)S(1)} %get-tuple-element.65) | copy-start | bytes 835588
  36.2 8.7 %copy-start.1 = (f32[544,544]{0,1:T(8,128)}, f32[544,544]{0,1:T(8,128)S(1)}, u32[]{:S(2)}) copy-start(f32[544,544]{0,1:T(8,128)S(1)} %get-tuple-element.61) | copy-start | bytes 3551236
  36.6 8.9 %copy-start.19 = (f32[128,544]{0,1:T(8,128)}, f32[128,544]{0,1:T(8,128)S(1)}, u32[]{:S(2)}) copy-start(f32[128,544]{0,1:T(8,128)S(1)} %get-tuple-element.59) | copy-start | bytes 835588
  37.5 9.0 %copy-start.4 = (f32[544,544]{0,1:T(8,128)}, f32[544,544]{0,1:T(8,128)S(1)}, u32[]{:S(2)}) copy-start(f32[544,544]{0,1:T(8,128)S(1)} %get-tuple-element.55) | copy-start | bytes 3551236
  37.8 9.1 %copy-start.21 = (f32[128,544]{0,1:T(8,128)}, f32[128,544]{0,1:T(8,128)S(1)}, u32[]{:S(2)}) copy-start(f32[128,544]{0,1:T(8,128)S(1)} %get-tuple-element.53) | copy-start | bytes 835588
  38.7 9.2 %copy-start.7 = (f32[544,544]{0,1:T(8,128)}, f32[544,544]{0,1:T(8,128)S(1)}, u32[]{:S(2)}) copy-start(f32[544,544]{0,1:T(8,128)S(1)} %get-tuple-element.49) | copy-start | bytes 3551236
  39.0 9.4 %copy-start.23 = (f32[128,544]{0,1:T(8,128)}, f32[128,544]{0,1:T(8,128)S(1)}, u32[]{:S(2)}) copy-start(f32[128,544]{0,1:T(8,128)S(1)} %get-tuple-element.47) | copy-start | bytes 835588
  39.9 9.5 %copy-start.10 = (f32[544,544]{0,1:T(8,128)}, f32[544,544]{0,1:T(8,128)S(1)}, u32[]{:S(2)}) copy-start(f32[544,544]{0,1:T(8,128)S(1)} %get-tuple-element.43) | copy-start | bytes 3551236
  40.3 9.7 %copy-start.25 = (f32[128,544]{0,1:T(8,128)}, f32[128,544]{0,1:T(8,128)S(1)}, u32[]{:S(2)}) copy-start(f32[128,544]{0,1:T(8,128)S(1)} %get-tuple-element.41) | copy-start | bytes 835588
  40.9 10.0 %copy-start.13 = (f32[544,544]{0,1:T(8,128)}, f32[544,544]{0,1:T(8,128)S(1)}, u32[]{:S(2)}) copy-start(f32[544,544]{0,1:T(8,128)S(1)} %get-tuple-element.37) | copy-start | bytes 3551236
  41.3 10.2 %copy-start.27 = (f32[128,544]{0,1:T(8,128)}, f32[128,544]{0,1:T(8,128)S(1)}, u32[]{:S(2)}) copy-start(f32[128,544]{0,1:T(8,128)S(1)} %get-tuple-element.35) | copy-start | bytes 835588
  56.1 6.2 %copy-start.14 = (f32[544,544]{0,1:T(8,128)S(1)}, f32[544,544]{0,1:T(8,128)}, u32[]{:S(2)}) copy-start(f32[544,544]{0,1:T(8,128)} %copy-done.13) | copy-start | bytes 3551236
  56.1 6.2 %copy-start.69 = (f32[544,128]{1,0:T(8,128)S(1)}, f32[544,128]{1,0:T(8,128)}, u32[]{:S(2)}) copy-start(f32[544,128]{1,0:T(8,128)} %fusion.241) | copy-start | bytes 835588
  56.1 6.2 %copy-start.108 = (f32[544]{0:T(1024)S(1)}, f32[544]{0:T(1024)}, u32[]{:S(2)}) copy-start(f32[544]{0:T(1024)} %copy-done.107) | copy-start | bytes 6532
  70.0 2.6 %copy-start.57 = (bf16[1,544,1,1,128]{4,1,3,2,0:T(8,128)(2,1)}, bf16[1,544,1,1,128]{4,1,3,2,0:T(8,128)(2,1)S(1)}, u32[]{:S(2)}) copy-start(bf16[1,544,1,1,128]{4,1,3,2,0:T(8,128)(2,1)S(1)} %get-tuple-element.15) | copy-start | bytes 417796
  70.1 3.1 %copy-start.114 = (f32[544]{0:T(1024)}, f32[544]{0:T(1024)S(1)}, u32[]{:S(2)}) copy-start(f32[544]{0:T(1024)S(1)} %get-tuple-element.8) | copy-start | bytes 6532
  70.1 3.4 %copy-start.53 = (bf16[1,544,1,1,128]{4,1,3,2,0:T(8,128)(2,1)}, bf16[1,544,1,1,128]{4,1,3,2,0:T(8,128)(2,1)S(1)}, u32[]{:S(2)}) copy-start(bf16[1,544,1,1,128]{4,1,3,2,0:T(8,128)(2,1)S(1)} %get-tuple-element.13) | copy-start | bytes 417796
  70.1 3.8 %copy-start.112 = (f32[544]{0:T(1024)}, f32[544]{0:T(1024)S(1)}, u32[]{:S(2)}) copy-start(f32[544]{0:T(1024)S(1)} %get-tuple-element.9) | copy-start | bytes 6532
  70.1 4.2 %copy-start.51 = (bf16[1,544,1,1,128]{4,1,3,2,0:T(8,128)(2,1)}, bf16[1,544,1,1,128]{4,1,3,2,0:T(8,128)(2,1)S(1)}, u32[]{:S(2)}) copy-start(bf16[1,544,1,1,128]{4,1,3,2,0:T(8,128)(2,1)S(1)} %get-tuple-element.12) | copy-start | bytes 417796
  70.1 4.6 %copy-start.110 = (f32[544]{0:T(1024)}, f32[544]{0:T(1024)S(1)}, u32[]{:S(2)}) copy-start(f32[544]{0:T(1024)S(1)} %get-tuple-element.10) | copy-start | bytes 6532
  70.1 4.9 %copy-start.49 = (bf16[1,544,1,1,128]{4,1,3,2,0:T(8,128)(2,1)}, bf16[1,544,1,1,128]{4,1,3,2,0:T(8,128)(2,1)S(1)}, u32[]{:S(2)}) copy-start(bf16[1,544,1,1,128]{4,1,3,2,0:T(8,128)(2,1)S(1)} %get-tuple-element.11) | copy-start | bytes 417796
  70.1 5.7 %copy-start.47 = (bf16[1,544,1,1,128]{4,1,3,2,0:T(8,128)(2,1)}, bf16[1,544,1,1,128]{4,1,3,2,0:T(8,128)(2,1)S(1)}, u32[]{:S(2)}) copy-start(bf16[1,544,1,1,128]{4,1,3,2,0:T(8,128)(2,1)S(1)} %get-tuple-element.17) | copy-start | bytes 417796
  71.9 4.4 %copy-start.77 = (bf16[544,128]{1,0:T(8,128)(2,1)}, bf16[544,128]{1,0:T(8,128)(2,1)S(1)}, u32[]{:S(2)}) copy-start(bf16[544,128]{1,0:T(8,128)(2,1)S(1)} %fusion.62) | copy-start | bytes 417796
  72.7 3.9 %copy-start.79 = (bf16[544,128]{1,0:T(8,128)(2,1)}, bf16[544,128]{1,0:T(8,128)(2,1)S(1)}, u32[]{:S(2)}) copy-start(bf16[544,128]{1,0:T(8,128)(2,1)S(1)} %fusion.63) | copy-start | bytes 417796
  73.5 3.4 %copy-start.81 = (bf16[544,128]{1,0:T(8,128)(2,1)}, bf16[544,128]{1,0:T(8,128)(2,1)S(1)}, u32[]{:S(2)}) copy-start(bf16[544,128]{1,0:T(8,128)(2,1)S(1)} %fusion.64) | copy-start | bytes 417796
  74.3 3.0 %copy-start.83 = (bf16[544,128]{1,0:T(8,128)(2,1)}, bf16[544,128]{1,0:T(8,128)(2,1)S(1)}, u32[]{:S(2)}) copy-start(bf16[544,128]{1,0:T(8,128)(2,1)S(1)} %fusion.65) | copy-start | bytes 417796
  77.8 3.0 %copy-start.121 = (f32[544]{0:T(1024)S(1)}, f32[544]{0:T(1024)}, u32[]{:S(2)}) copy-start(f32[544]{0:T(1024)} %copy-done.120) | copy-start | bytes 6532
  (97 other events, 142.2 us)
Sparse Core Ops, SparseCore 0:
  79.0 20.4 reduce-scatter.3
where the time goes:
time: 113 us; the launch traced here: 112 us
  matrix products  40 us (35%)
  local copies, waits for them, and re-layouts  31.5 us (28%)
  between operations  18.1 us (16%)
  blocking collectives  15.1 us (13%)
  other arithmetic  7.4 us (7%)
    dot_general x84, matrix products, product(): jnp.einsum(pattern, first_arg, second_arg, preferred_element_type=jnp.flo...  40 us
    unnamed x269, local copies, waits for them, and re-layouts  15.5 us
    all_gather x1, blocking collectives, local(): beacon_pairs = lax.all_gather(own_pair, 'span', axis=0, tiled=True)  15.1 us
    slice x1, local copies, waits for them, and re-layouts, local(): grad_blocks[:, :, 0, head_index]  6.13 us
    reshape x1, local copies, waits for them, and re-layouts, local(): grad_blocks = out_grad.reshape(local_spans, SEG, groups, QPG, HD)  3.03 us
    slice x1, local copies, waits for them, and re-layouts, local(): query_blocks[:, :, 0, head_index]  2.37 us
  transfers between devices with their start and end apart: 1, of which 0 were waited for; matrix products, arithmetic and copies ran while one was open for 16% of the time, Pallas kernels for 0%

commit v1 on v0

--- a/solution.py
+++ b/solution.py
@@ -116,7 +116,10 @@
         ],
         1,
     )
-    beacon_pairs = lax.all_gather(own_pair, "span", axis=0, tiled=True)
+    size = lax.axis_size("span")
+    blocks = jnp.stack([own_pair for _ in range(size)])
+    blocks = lax.all_to_all(blocks, "span", split_axis=0, concat_axis=0)
+    beacon_pairs = jnp.concatenate(blocks, axis=0)
     attended_parts, query_parts, term_keys, term_values, own_key_parts, own_value_parts = (
         [],
         [],

time: 113 us -> 129 us (1.14)
  matrix products: 40 us -> 59 us
  blocking collectives: 15.1 us -> 0 us
  waiting for transfers between devices: 0.04 us -> 10.3 us
  starting transfers between devices: 0.04 us -> 6.35 us
  local copies, waits for them, and re-layouts: 31.5 us -> 26.7 us
    dot_general x84, matrix products: 40 us -> 59 us  [product(): jnp.einsum(pattern, first_arg, second_arg, preferred_element_type=jnp.flo...]
    all_gather x1 -> x0, blocking collectives: 15.1 us -> none  [local(): beacon_pairs = lax.all_gather(own_pair, 'span', axis=0, tiled=True)]
    unnamed x2, waiting for transfers between devices: 0.04 us -> 10.3 us
    unnamed x269 -> x129, local copies, waits for them, and re-layouts: 15.5 us -> 8.1 us
    all_to_all x0 -> x1, starting transfers between devices: none -> 6.35 us  [local(): blocks = lax.all_to_all(blocks, 'span', split_axis=0, concat_axis=0)]
  transfers between devices with their start and end apart: 1 -> 2, of which waited for: 0 -> 1; matrix products, arithmetic and copies ran while one was open for 16% -> 33% of each run, Pallas kernels for 0% -> 0%
where the time goes in v1:
time: 129 us; the launch traced here: 128 us
  matrix products  59 us (46%)
  local copies, waits for them, and re-layouts  26.7 us (21%)
  between operations  17.2 us (13%)
  waiting for transfers between devices  10.3 us (8%)
  other arithmetic  8.68 us (7%)
  starting transfers between devices  6.35 us (5%)
    dot_general x84, matrix products, product(): jnp.einsum(pattern, first_arg, second_arg, preferred_element_type=jnp.flo...  59 us
    unnamed x2, waiting for transfers between devices  10.3 us
    unnamed x129, local copies, waits for them, and re-layouts  8.1 us
    slice x1, local copies, waits for them, and re-layouts, local(): grad_blocks[:, :, 0, head_index]  6.81 us
    all_to_all x1, starting transfers between devices, local(): blocks = lax.all_to_all(blocks, 'span', split_axis=0, concat_axis=0)  6.35 us
    reshape x1, local copies, waits for them, and re-layouts, local(): grad_blocks = out_grad.reshape(local_spans, SEG, groups, QPG, HD)  2.98 us
  transfers between devices with their start and end apart: 2, of which 1 were waited for; matrix products, arithmetic and copies ran while one was open for 33% of the time, Pallas kernels for 0%

profile of v1, /device:TPU:0, one launch (start us, length us, event | category | flops | bytes accessed | tf_op | source)
XLA Modules:
  0.0 128.3 jit_solution(9557685229472989318)
XLA Ops:
  8.5 6.3 %all-to-all-start = ((bf16[4,32,256]{2,1,0:T(8,128)(2,1)}), bf16[4,32,256]{2,1,0:T(8,128)(2,1)S(1)}, u32[]{:S(2)}, u32[]{:S(2)}) async-start(bf16[4,32,256]{2,1,0:T(8,128)(2,1)} %stack.61), calls=%async_computation | async-start | bytes 131072 | tf_op jit(solution)/shard_map/all_to_all | solution.py:121
  14.9 1.2 dynamic_slice.3
  19.6 2.2 %reshape.1314 = bf16[1,544,1,7,128]{4,3,1,2,0:T(8,128)(2,1)S(1)} reshape(bf16[544,896]{1,0:T(8,128)(2,1)} %param.5) | data formatting | bytes 1949696 | tf_op jit(solution)/shard_map/reshape | solution.py:108
  21.8 2.4 %fusion.265 = (bf16[1,544,1,1,128]{4,3,1,2,0:T(2,128)(2,1)S(1)}, bf16[1,544,1,1,128]{4,3,1,2,0:T(2,128)(2,1)S(1)}, bf16[1,544,1,1,128]{4,3,1,2,0:T(2,128)(2,1)},...) fusion(bf16[1,544,1,7,128]{4,3,1,2,0:T(8,128)(2,1)S(1)} %reshap, ...), kind=kLoop, calls=%fused_computation.404 | loop fusion | bytes 1949696 | tf_op jit(solution)/shard_map/slice | solution.py:143
  24.9 1.2 fusion.280
  26.2 1.2 fusion.278
  27.4 2.5 %fusion.276 = (f32[544]{0:T(1024)}, f32[544,544]{0,1:T(8,128)}) fusion(bf16[544,128]{1,0:T(8,128)(2,1)S(1)} %copy-done.6, bf16[1,544,1,1,128]{4,1,3,2,0:T(8,128)(2,1)S(1)} %copy.70, pred[544]{0:T(1024)(128)(4,1)S(1)} %get-tuple-element.81, pred[544]{0:T(1024)(128)(4,1)S(1)} %get-tuple-element.80, s32[544]{0:T(1024)S(1)} %iota_select_fusion, ...), kind=kOutput, calls=%fused_computation.415 | convolution fusion | flops 78718432 | bytes 1468256 | tf_op jit(solution)/shard_map/csd,ctd->cst/dot_general | solution.py:15
  30.0 3.5 %fusion.274 = (f32[544]{0:T(1024)}, f32[544,544]{0,1:T(8,128)}) fusion(bf16[544,128]{1,0:T(8,128)(2,1)S(1)} %copy-done.6, bf16[1,544,1,1,128]{4,1,3,2,0:T(8,128)(2,1)S(1)} %copy.69, pred[544]{0:T(1024)(128)(4,1)} %copy-done.54, pred[544]{0:T(1024)(128)(4,1)S(1)} %get-tuple-element.80, s32[544]{0:T(1024)S(1)} %iota_select_fusion, pred[544]{0:T(1024)(128)(4,1)} %copy-done.56), kind=kOutput, calls=%fused_computation.413 | convolution fusion | flops 78718432 | bytes 1468256 | tf_op jit(solution)/shard_map/csd,ctd->cst/dot_general | solution.py:15
  33.5 2.5 %fusion.272 = (f32[544]{0:T(1024)}, f32[544,544]{0,1:T(8,128)}) fusion(bf16[544,128]{1,0:T(8,128)(2,1)S(1)} %copy-done.6, bf16[1,544,1,1,128]{4,1,3,2,0:T(8,128)(2,1)S(1)} %copy.68, pred[544]{0:T(1024)(128)(4,1)S(1)} %copy-done.55, pred[544]{0:T(1024)(128)(4,1)S(1)} %get-tuple-element.80, s32[544]{0:T(1024)S(1)} %iota_select_fusion, ...), kind=kOutput, calls=%fused_computation.411 | convolution fusion | flops 78718432 | bytes 1468256 | tf_op jit(solution)/shard_map/csd,ctd->cst/dot_general | solution.py:15
  36.1 2.5 %fusion.270 = (f32[544]{0:T(1024)}, f32[544,544]{0,1:T(8,128)}) fusion(bf16[544,128]{1,0:T(8,128)(2,1)S(1)} %copy-done.6, bf16[1,544,1,1,128]{4,1,3,2,0:T(8,128)(2,1)S(1)} %copy.67, pred[544]{0:T(1024)(128)(4,1)S(1)} %copy-done.55, pred[544]{0:T(1024)(128)(4,1)S(1)} %get-tuple-element.80, s32[544]{0:T(1024)S(1)} %iota_select_fusion, ...), kind=kOutput, calls=%fused_computation.409 | convolution fusion | flops 78718432 | bytes 1468256 | tf_op jit(solution)/shard_map/csd,ctd->cst/dot_general | solution.py:15
  38.6 2.5 %fusion.268 = (f32[544]{0:T(1024)}, f32[544,544]{0,1:T(8,128)}) fusion(bf16[544,128]{1,0:T(8,128)(2,1)S(1)} %copy-done.6, bf16[1,544,1,1,128]{4,1,3,2,0:T(8,128)(2,1)S(1)} %copy.66, pred[544]{0:T(1024)(128)(4,1)S(1)} %copy-done.55, pred[544]{0:T(1024)(128)(4,1)S(1)} %get-tuple-element.80, s32[544]{0:T(1024)S(1)} %iota_select_fusion, ...), kind=kOutput, calls=%fused_computation.407 | convolution fusion | flops 78718432 | bytes 1468256 | tf_op jit(solution)/shard_map/csd,ctd->cst/dot_general | solution.py:15
  41.1 3.0 %reshape.1322 = bf16[1,544,1,7,128]{4,3,1,2,0:T(8,128)(2,1)} reshape(bf16[544,896]{1,0:T(8,128)(2,1)} %param.8) | data formatting | bytes 1949696 | tf_op jit(solution)/shard_map/reshape | solution.py:109
  44.1 6.8 %fusion.264 = (bf16[1,544,1,1,128]{4,3,1,2,0:T(2,128)(2,1)}, bf16[1,544,1,1,128]{4,3,1,2,0:T(2,128)(2,1)}, bf16[1,544,1,1,128]{4,3,1,2,0:T(2,128)(2,1)}, bf16[1,...) fusion(bf16[1,544,1,7,128]{4,3,1,2,0:T(8,128)(2,1)} %reshape.1322), kind=kLoop, calls=%fused_computation.403 | loop fusion | bytes 1949696 | tf_op jit(solution)/shard_map/slice | solution.py:144
  51.0 1.0 fusion.279
  52.0 1.0 fusion.277
  52.9 1.0 fusion.275
  53.9 1.0 fusion.273
  54.9 1.0 fusion.271
  55.9 1.0 fusion.269
  56.8 1.0 fusion.267
  67.8 0.9 copy-done.24
  68.7 0.9 multiply_reduce_fusion
  70.9 1.3 %fusion.22 = bf16[544,544]{0,1:T(8,128)(2,1)} fusion(bf16[544,128]{1,0:T(8,128)(2,1)S(1)} %copy-done, f32[544,544]{0,1:T(8,128)S(1)} %copy-done.5, f32[544]{0:T(1024)S(1)} %get-tuple-element.5, f32[544]{0:T(1024)S(1)} %log_add_fusion.6, bf16[1,544,1,1,128]{4,1,3,2,0:T(8,128)(2,1)S(1)} %get-tuple-element.16, bf16[544]{0:T(1024)(128)(2,1)S(1)} %get-tuple-element.76), kind=kOutput, calls=%fused_computation.51 | convolution fusion | flops 77012992 | bytes 2059584 | tf_op jit(solution)/shard_map/csd,ctd->cst/dot_general | solution.py:15
  72.5 1.3 %fusion.21 = bf16[544,544]{0,1:T(8,128)(2,1)} fusion(bf16[544,128]{1,0:T(8,128)(2,1)S(1)} %copy-done, f32[544,544]{0,1:T(8,128)S(1)} %copy-done.4, f32[544]{0:T(1024)S(1)} %get-tuple-element.6, f32[544]{0:T(1024)S(1)} %log_add_fusion.5, bf16[1,544,1,1,128]{4,1,3,2,0:T(8,128)(2,1)S(1)} %get-tuple-element.15, bf16[544]{0:T(1024)(128)(2,1)S(1)} %get-tuple-element.76), kind=kOutput, calls=%fused_computation.50 | convolution fusion | flops 77012992 | bytes 2059584 | tf_op jit(solution)/shard_map/csd,ctd->cst/dot_general | solution.py:15
  74.1 1.3 %fusion.20 = bf16[544,544]{0,1:T(8,128)(2,1)} fusion(bf16[544,128]{1,0:T(8,128)(2,1)S(1)} %copy-done, f32[544,544]{0,1:T(8,128)S(1)} %copy-done.3, f32[544]{0:T(1024)S(1)} %get-tuple-element.7, f32[544]{0:T(1024)S(1)} %log_add_fusion.4, bf16[1,544,1,1,128]{4,1,3,2,0:T(8,128)(2,1)S(1)} %get-tuple-element.14, bf16[544]{0:T(1024)(128)(2,1)S(1)} %get-tuple-element.76), kind=kOutput, calls=%fused_computation.49 | convolution fusion | flops 77012992 | bytes 2059584 | tf_op jit(solution)/shard_map/csd,ctd->cst/dot_general | solution.py:15
  76.0 1.3 %fusion.19 = bf16[544,544]{0,1:T(8,128)(2,1)} fusion(bf16[544,128]{1,0:T(8,128)(2,1)S(1)} %copy-done, f32[544,544]{0,1:T(8,128)S(1)} %copy-done.2, f32[544]{0:T(1024)S(1)} %get-tuple-element.8, f32[544]{0:T(1024)S(1)} %log_add_fusion.3, bf16[1,544,1,1,128]{4,1,3,2,0:T(8,128)(2,1)S(1)} %get-tuple-element.13, bf16[544]{0:T(1024)(128)(2,1)S(1)} %get-tuple-element.76), kind=kOutput, calls=%fused_computation.48 | convolution fusion | flops 77012992 | bytes 2059584 | tf_op jit(solution)/shard_map/csd,ctd->cst/dot_general | solution.py:15
  77.6 1.4 %fusion.18 = bf16[544,544]{0,1:T(8,128)(2,1)} fusion(bf16[544,128]{1,0:T(8,128)(2,1)S(1)} %copy-done, f32[544,544]{0,1:T(8,128)S(1)} %copy-done.1, f32[544]{0:T(1024)S(1)} %get-tuple-element.9, f32[544]{0:T(1024)S(1)} %log_add_fusion.2, bf16[1,544,1,1,128]{4,1,3,2,0:T(8,128)(2,1)S(1)} %get-tuple-element.12, bf16[544]{0:T(1024)(128)(2,1)S(1)} %get-tuple-element.76), kind=kOutput, calls=%fused_computation.47 | convolution fusion | flops 77012992 | bytes 2059584 | tf_op jit(solution)/shard_map/csd,ctd->cst/dot_general | solution.py:15
  79.3 1.3 %fusion.17 = bf16[544,544]{0,1:T(8,128)(2,1)} fusion(bf16[544,128]{1,0:T(8,128)(2,1)S(1)} %copy-done, f32[544,544]{0,1:T(8,128)S(1)} %get-tuple-element.67, f32[544]{0:T(1024)S(1)} %get-tuple-element.10, f32[544]{0:T(1024)S(1)} %log_add_fusion.1, bf16[1,544,1,1,128]{4,1,3,2,0:T(8,128)(2,1)S(1)} %get-tuple-element.11, bf16[544]{0:T(1024)(128)(2,1)S(1)} %get-tuple-element.76), kind=kOutput, calls=%fused_computation.46 | convolution fusion | flops 77012992 | bytes 2059584 | tf_op jit(solution)/shard_map/csd,ctd->cst/dot_general | solution.py:15
  80.9 1.3 %fusion.16 = bf16[544,544]{0,1:T(8,128)(2,1)} fusion(bf16[544,128]{1,0:T(8,128)(2,1)S(1)} %copy-done, f32[544,544]{0,1:T(8,128)S(1)} %get-tuple-element.73, f32[544]{0:T(1024)S(1)} %get-tuple-element.4, f32[544]{0:T(1024)S(1)} %log_add_fusion, bf16[1,544,1,1,128]{4,1,3,2,0:T(8,128)(2,1)S(1)} %get-tuple-element.17, bf16[544]{0:T(1024)(128)(2,1)S(1)} %get-tuple-element.76), kind=kOutput, calls=%fused_computation.45 | convolution fusion | flops 77012992 | bytes 2059584 | tf_op jit(solution)/shard_map/csd,ctd->cst/dot_general | solution.py:15
  105.0 1.1 copy.93
  106.9 1.1 copy.94
  108.0 10.3 %reduce-scatter.4.cloned.1.call-done = f32[32,256]{1,0:T(8,128)} async-done(((f32[128,256]{1,0:T(8,128)}), f32[32,256]{1,0:T(8,128)}) %reduce-scatter.4.cloned.1.call-update) | async-done | bytes 32784
  (241 shorter events, 42.8 us)
Async XLA Ops:
  8.5 42.4 %all-to-all-start = ((bf16[4,32,256]{2,1,0:T(8,128)(2,1)}), bf16[4,32,256]{2,1,0:T(8,128)(2,1)S(1)}, u32[]{:S(2)}, u32[]{:S(2)}) async-start(bf16[4,32,256]{2,1,0:T(8,128)(2,1)} %stack.61), calls=%async_computation | async-start | bytes 131072 | tf_op jit(solution)/shard_map/all_to_all | solution.py:121
  14.9 103.5 %reduce-scatter.4.cloned.1.call-start = ((), (), s32[]{:S(2)}) async-start(), calls=%async_computation.2 | async-start | bytes 163840
  18.1 9.3 %copy-start.56 = (pred[544]{0:T(1024)(128)(4,1)}, pred[544]{0:T(1024)(128)(4,1)S(1)}, u32[]{:S(2)}) copy-start(pred[544]{0:T(1024)(128)(4,1)S(1)} %fusion.220) | copy-start | bytes 1636
  18.9 8.5 %copy-start.54 = (pred[544]{0:T(1024)(128)(4,1)}, pred[544]{0:T(1024)(128)(4,1)S(1)}, u32[]{:S(2)}) copy-start(pred[544]{0:T(1024)(128)(4,1)S(1)} %get-tuple-element.81) | copy-start | bytes 1636
  21.8 3.2 %copy-start.6 = (bf16[544,128]{1,0:T(8,128)(2,1)S(1)}, bf16[544,128]{1,0:T(8,128)(2,1)}, u32[]{:S(2)}) copy-start(bf16[544,128]{1,0:T(8,128)(2,1)} %param.6) | copy-start | bytes 417796
  27.4 2.5 %copy-start.43 = (bf16[1,544,1,1,128]{4,3,1,2,0:T(2,128)(2,1)S(1)}, bf16[1,544,1,1,128]{4,3,1,2,0:T(2,128)(2,1)}, u32[]{:S(2)}) copy-start(bf16[1,544,1,1,128]{4,3,1,2,0:T(2,128)(2,1)} %get-tuple-element.28) | copy-start | bytes 417796
  29.9 3.5 %copy-start.15 = (bf16[1,544,1,1,128]{4,1,3,2,0:T(8,128)(2,1)}, bf16[1,544,1,1,128]{4,1,3,2,0:T(8,128)(2,1)S(1)}, u32[]{:S(2)}) copy-start(bf16[1,544,1,1,128]{4,1,3,2,0:T(8,128)(2,1)S(1)} %copy.69) | copy-start | bytes 417796
  30.0 3.5 %copy-start.42 = (bf16[1,544,1,1,128]{4,3,1,2,0:T(2,128)(2,1)S(1)}, bf16[1,544,1,1,128]{4,3,1,2,0:T(2,128)(2,1)}, u32[]{:S(2)}) copy-start(bf16[1,544,1,1,128]{4,3,1,2,0:T(2,128)(2,1)} %get-tuple-element.29) | copy-start | bytes 417796
  30.0 3.5 %copy-start.55 = (pred[544]{0:T(1024)(128)(4,1)S(1)}, pred[544]{0:T(1024)(128)(4,1)}, u32[]{:S(2)}) copy-start(pred[544]{0:T(1024)(128)(4,1)} %copy-done.54) | copy-start | bytes 1636
  30.0 3.5 %copy-start.57 = (pred[544]{0:T(1024)(128)(4,1)S(1)}, pred[544]{0:T(1024)(128)(4,1)}, u32[]{:S(2)}) copy-start(pred[544]{0:T(1024)(128)(4,1)} %copy-done.56) | copy-start | bytes 1636
  33.5 2.5 %copy-start.18 = (bf16[1,544,1,1,128]{4,1,3,2,0:T(8,128)(2,1)}, bf16[1,544,1,1,128]{4,1,3,2,0:T(8,128)(2,1)S(1)}, u32[]{:S(2)}) copy-start(bf16[1,544,1,1,128]{4,1,3,2,0:T(8,128)(2,1)S(1)} %copy.68) | copy-start | bytes 417796
  33.5 2.5 %copy-start.41 = (bf16[1,544,1,1,128]{4,3,1,2,0:T(2,128)(2,1)S(1)}, bf16[1,544,1,1,128]{4,3,1,2,0:T(2,128)(2,1)}, u32[]{:S(2)}) copy-start(bf16[1,544,1,1,128]{4,3,1,2,0:T(2,128)(2,1)} %get-tuple-element.30) | copy-start | bytes 417796
  36.1 2.5 %copy-start.21 = (bf16[1,544,1,1,128]{4,1,3,2,0:T(8,128)(2,1)}, bf16[1,544,1,1,128]{4,1,3,2,0:T(8,128)(2,1)S(1)}, u32[]{:S(2)}) copy-start(bf16[1,544,1,1,128]{4,1,3,2,0:T(8,128)(2,1)S(1)} %copy.67) | copy-start | bytes 417796
  36.1 2.5 %copy-start.40 = (bf16[1,544,1,1,128]{4,3,1,2,0:T(2,128)(2,1)S(1)}, bf16[1,544,1,1,128]{4,3,1,2,0:T(2,128)(2,1)}, u32[]{:S(2)}) copy-start(bf16[1,544,1,1,128]{4,3,1,2,0:T(2,128)(2,1)} %get-tuple-element.31) | copy-start | bytes 417796
  50.9 3.0 %copy-start.16 = (bf16[1,544,1,1,128]{4,1,3,2,0:T(8,128)(2,1)S(1)}, bf16[1,544,1,1,128]{4,1,3,2,0:T(8,128)(2,1)}, u32[]{:S(2)}) copy-start(bf16[1,544,1,1,128]{4,1,3,2,0:T(8,128)(2,1)} %copy-done.15) | copy-start | bytes 417796
  50.9 3.9 %copy-start.19 = (bf16[1,544,1,1,128]{4,1,3,2,0:T(8,128)(2,1)S(1)}, bf16[1,544,1,1,128]{4,1,3,2,0:T(8,128)(2,1)}, u32[]{:S(2)}) copy-start(bf16[1,544,1,1,128]{4,1,3,2,0:T(8,128)(2,1)} %copy-done.18) | copy-start | bytes 417796
  51.0 4.9 %copy-start.22 = (bf16[1,544,1,1,128]{4,1,3,2,0:T(8,128)(2,1)S(1)}, bf16[1,544,1,1,128]{4,1,3,2,0:T(8,128)(2,1)}, u32[]{:S(2)}) copy-start(bf16[1,544,1,1,128]{4,1,3,2,0:T(8,128)(2,1)} %copy-done.21) | copy-start | bytes 417796
  52.0 5.8 %copy-start.53 = (f32[544]{0:T(1024)S(1)}, f32[544]{0:T(1024)}, u32[]{:S(2)}) copy-start(f32[544]{0:T(1024)} %get-tuple-element.72) | copy-start | bytes 6532
  56.8 1.8 %copy-start.52 = (f32[544]{0:T(1024)S(1)}, f32[544]{0:T(1024)}, u32[]{:S(2)}) copy-start(f32[544]{0:T(1024)} %get-tuple-element.66) | copy-start | bytes 6532
  67.2 1.5 %copy-start.33 = (bf16[1,544,1,1,128]{4,3,1,2,0:T(2,128)(2,1)S(1)}, bf16[1,544,1,1,128]{4,3,1,2,0:T(2,128)(2,1)}, u32[]{:S(2)}) copy-start(bf16[1,544,1,1,128]{4,3,1,2,0:T(2,128)(2,1)} %get-tuple-element.18) | copy-start | bytes 417796
  67.2 1.5 %copy-start.34 = (bf16[1,544,1,1,128]{4,3,1,2,0:T(2,128)(2,1)S(1)}, bf16[1,544,1,1,128]{4,3,1,2,0:T(2,128)(2,1)}, u32[]{:S(2)}) copy-start(bf16[1,544,1,1,128]{4,3,1,2,0:T(2,128)(2,1)} %get-tuple-element.19) | copy-start | bytes 417796
  67.2 1.5 %copy-start.35 = (bf16[1,544,1,1,128]{4,3,1,2,0:T(2,128)(2,1)S(1)}, bf16[1,544,1,1,128]{4,3,1,2,0:T(2,128)(2,1)}, u32[]{:S(2)}) copy-start(bf16[1,544,1,1,128]{4,3,1,2,0:T(2,128)(2,1)} %get-tuple-element.20) | copy-start | bytes 417796
  67.2 1.5 %copy-start.36 = (bf16[1,544,1,1,128]{4,3,1,2,0:T(2,128)(2,1)S(1)}, bf16[1,544,1,1,128]{4,3,1,2,0:T(2,128)(2,1)}, u32[]{:S(2)}) copy-start(bf16[1,544,1,1,128]{4,3,1,2,0:T(2,128)(2,1)} %get-tuple-element.21) | copy-start | bytes 417796
  67.2 1.5 %copy-start.37 = (bf16[1,544,1,1,128]{4,3,1,2,0:T(2,128)(2,1)S(1)}, bf16[1,544,1,1,128]{4,3,1,2,0:T(2,128)(2,1)}, u32[]{:S(2)}) copy-start(bf16[1,544,1,1,128]{4,3,1,2,0:T(2,128)(2,1)} %get-tuple-element.22) | copy-start | bytes 417796
  67.3 1.5 %copy-start.38 = (bf16[1,544,1,1,128]{4,3,1,2,0:T(2,128)(2,1)S(1)}, bf16[1,544,1,1,128]{4,3,1,2,0:T(2,128)(2,1)}, u32[]{:S(2)}) copy-start(bf16[1,544,1,1,128]{4,3,1,2,0:T(2,128)(2,1)} %get-tuple-element.23) | copy-start | bytes 417796
  67.3 1.5 %copy-start.39 = (bf16[1,544,1,1,128]{4,3,1,2,0:T(2,128)(2,1)S(1)}, bf16[1,544,1,1,128]{4,3,1,2,0:T(2,128)(2,1)}, u32[]{:S(2)}) copy-start(bf16[1,544,1,1,128]{4,3,1,2,0:T(2,128)(2,1)} %get-tuple-element.24) | copy-start | bytes 417796
  86.1 4.2 %copy-start.45 = (f32[1,544,1,128]{3,1,2,0:T(8,128)}, f32[1,544,1,128]{3,1,2,0:T(8,128)S(1)}, u32[]{:S(2)}) copy-start(f32[1,544,1,128]{3,1,2,0:T(8,128)S(1)} %fusion.30) | copy-start | bytes 835588
  94.7 2.6 %copy-start.7 = (bf16[544,544]{0,1:T(8,128)(2,1)S(1)}, bf16[544,544]{0,1:T(8,128)(2,1)}, u32[]{:S(2)}) copy-start(bf16[544,544]{0,1:T(8,128)(2,1)} %fusion.22) | copy-start | bytes 1775620
  95.6 2.1 %copy-start.26 = (f32[544,128]{1,0:T(8,128)S(1)}, f32[544,128]{1,0:T(8,128)}, u32[]{:S(2)}) copy-start(f32[544,128]{1,0:T(8,128)} %fusion.255) | copy-start | bytes 835588
  96.5 1.6 %copy-start.13 = (bf16[544,544]{0,1:T(8,128)(2,1)S(1)}, bf16[544,544]{0,1:T(8,128)(2,1)}, u32[]{:S(2)}) copy-start(bf16[544,544]{0,1:T(8,128)(2,1)} %fusion.21) | copy-start | bytes 1775620
  96.5 1.6 %copy-start.23 = (bf16[1,544,1,1,128]{4,1,3,2,0:T(8,128)(2,1)S(1)}, bf16[1,544,1,1,128]{4,1,3,2,0:T(8,128)(2,1)}, u32[]{:S(2)}) copy-start(bf16[1,544,1,1,128]{4,1,3,2,0:T(8,128)(2,1)} %copy-done.21) | copy-start | bytes 417796
  106.9 13.2 %copy-start.46 = (bf16[512,128]{1,0:T(8,128)(2,1)S(1)}, bf16[512,128]{1,0:T(8,128)(2,1)}, u32[]{:S(2)}) copy-start(bf16[512,128]{1,0:T(8,128)(2,1)} %fusion.165) | copy-start | bytes 393220
  (28 other events, 33.9 us)
Sparse Core Ops, SparseCore 0:
  97.4 20.8 reduce-scatter.3
